TPU v7x, 32 devices: a whole 2x2x4 slice. The times are simulated.
32 devices in a mesh: row: 4 (over x, core), col: 8 (over z, y).
Axes of the slice: x: 2, y: 2, z: 4, core: 2. Of those that a mesh axis runs over, the one named last changes fastest.
Arguments:
- markov: bfloat16 [2, 256, 128, 128], P(None, 'col'), may hold values from -6 to 6
- omega: bfloat16 [32768, 64], P('col'), may hold values from -0.03125 to 0.03125
Outputs:
- denoised: float32 [2, 256, 128, 128], P(None, 'col')
All inputs are finite; a program needn't handle non-finite values.
Results may differ from a plain program's by a relative error of at most 0.0007.
Values may be sent and summed in bfloat16 or wider, within the bound.
No kernel may reach another device: no remote copies, remote signals or barrier semaphores. Data moves between devices by JAX's collectives and lax.ppermute only.
A program may use at most 64 MiB of HBM per device.

v0:
```python
import jax
import jax.numpy as jnp
from jax import lax
from jax.sharding import PartitionSpec as P

NS_STEPS = 8
norm_floor = 1e-06
highest = lax.Precision.HIGHEST


def shifted(block, axis, distance):
    devices = range(lax.axis_size(axis))
    route = [((i - distance) % len(devices), i) for i in devices]
    return lax.ppermute(block, axis, route)


def column_gram(matrix):
    return lax.dot_general(
        matrix,
        matrix,
        (((0,), (0,)), ((), ())),
        precision=highest,
        preferred_element_type=jnp.float32,
    )


def square_mul(left, right):
    return jnp.dot(left, right, precision=highest, preferred_element_type=jnp.float32)


def total_gram(partial_value):
    return lax.psum(partial_value, "row")


def orthonormal(sketch):
    gram = total_gram(column_gram(sketch))
    scale = 1.0 / jnp.sqrt(jnp.trace(gram) + norm_floor)
    coeffs = jnp.eye(gram.shape[0], dtype=jnp.float32) * scale
    for sweep in range(NS_STEPS):
        inner = square_mul(square_mul(coeffs.T, gram), coeffs)
        coeffs = 1.5 * coeffs - 0.5 * square_mul(coeffs, inner)
    return square_mul(sketch, coeffs)


def pick_half(pair, half_id):
    return jnp.where(half_id == 0, pair[0], pair[1])


def lag_sums(basis_blocks, column_rows, column_count):
    row_count, out_rows, rank_extent = basis_blocks.shape
    input_columns = column_rows.shape[1] // column_count
    start_total = jnp.zeros((out_rows, row_count + column_count, input_columns), jnp.float32)

    def add_row(row_position, running):
        orthonormal_row_vector = lax.dynamic_index_in_dim(
            basis_blocks, row_position, 0, keepdims=False
        )
        product = jnp.dot(orthonormal_row_vector, column_rows, preferred_element_type=jnp.float32)
        product = product.reshape(out_rows, column_count, input_columns)
        current_sum = lax.dynamic_slice_in_dim(running, row_position, column_count, 1)
        return lax.dynamic_update_slice_in_dim(running, current_sum + product, row_position, 1)

    return lax.fori_loop(0, row_count, add_row, start_total)


def local(markov, omega):
    n_rows = lax.axis_size("row")
    n_cols = lax.axis_size("col")
    row_position = lax.axis_index("row")
    col_id = lax.axis_index("col")
    halves, blocks, out_rows, input_columns = markov.shape
    rank_extent = omega.shape[1]
    bit_count = (n_rows - 1).bit_length()
    held = markov
    for bit_pos in range(bit_count):
        moved = shifted(held, "col", -(1 << bit_pos))
        held = jnp.where(row_position // (1 << bit_pos) % 2 == 1, moved, held)
    following = shifted(held, "col", -1)
    first_block = row_position + col_id
    window = jnp.concatenate(
        [pick_half(held, first_block // n_cols), pick_half(following, (first_block + 1) // n_cols)],
        axis=0,
    )
    omega_blocks = omega.reshape(blocks, input_columns, rank_extent)

    def slab_at(column_id):
        return lax.dynamic_slice_in_dim(window, column_id, blocks, 0).reshape(
            blocks * out_rows, input_columns
        )

    def range_step(column_id, running):
        weights = lax.dynamic_index_in_dim(omega_blocks, column_id, 0, keepdims=False)
        return running + jnp.dot(slab_at(column_id), weights, preferred_element_type=jnp.float32)

    partial_value = lax.fori_loop(
        0, blocks, range_step, jnp.zeros((blocks * out_rows, rank_extent), jnp.float32)
    )
    sketch = lax.psum(partial_value, "col")
    basis = orthonormal(sketch).astype(jnp.bfloat16)

    def projection_update(column_id, running):
        term = lax.dot_general(
            basis, slab_at(column_id), (((0,), (0,)), ((), ())), preferred_element_type=jnp.float32
        )
        return lax.dynamic_update_slice_in_dim(running, term, column_id * input_columns, 1)

    projected_matrix = lax.fori_loop(
        0, blocks, projection_update, jnp.zeros((rank_extent, blocks * input_columns), jnp.float32)
    )
    projected_matrix = lax.psum(projected_matrix, "row").astype(jnp.bfloat16)
    basis_blocks = basis.reshape(blocks, out_rows, rank_extent)
    local_sums = lag_sums(basis_blocks, projected_matrix, blocks).transpose(1, 0, 2)
    for bit_pos in range(bit_count):
        moved = shifted(local_sums.astype(jnp.bfloat16), "col", 1 << bit_pos).astype(
            local_sums.dtype
        )
        local_sums = jnp.where(row_position // (1 << bit_pos) % 2 == 1, moved, local_sums)
    carried = shifted(local_sums[blocks:].astype(jnp.bfloat16), "col", 1).astype(jnp.float32)
    own_half = (col_id < row_position).astype(jnp.int32)
    prev_col = (col_id + n_cols - 1) % n_cols
    carry_half = (prev_col + n_cols * (prev_col < row_position).astype(jnp.int32) + 1) // n_cols
    owned = jnp.stack(
        [
            jnp.where(own_half == half_id, local_sums[:blocks], 0.0)
            + jnp.where(carry_half == half_id, carried, 0.0)
            for half_id in range(2)
        ]
    )
    totals = lax.psum(owned, "row")
    total_rows = blocks * n_rows
    total_cols = blocks * n_cols
    lag_ids = (
        jnp.arange(2, dtype=jnp.int32)[:, None] * total_cols
        + col_id * blocks
        + jnp.arange(blocks, dtype=jnp.int32)[None, :]
    )
    counts = jnp.maximum(
        jnp.minimum(lag_ids, total_rows - 1) - jnp.maximum(0, lag_ids - total_cols + 1) + 1, 0
    )
    counts_f = counts.astype(jnp.float32)[:, :, None, None]
    measured = markov.astype(jnp.float32)
    averaged = totals / jnp.maximum(counts_f, 1.0)
    return jnp.where(counts_f > 0, 0.5 * measured + 0.5 * averaged, measured)


def solution(mesh):
    in_specs = (P(None, "col", None, None), P("col", None))
    out_specs = P(None, "col", None, None)
    return jax.shard_map(local, mesh=mesh, in_specs=in_specs, out_specs=out_specs, check_vma=False)
```

profile of v0, /device:TPU:0, one launch (start us, length us, event | category | flops | bytes accessed | tf_op | source)
XLA Modules:
  0.0 767.1 jit_solution(6744331033921523730)
XLA Ops:
  6.5 6.0 collective-permute-start
  12.6 45.2 %collective-permute-done = bf16[2,32,128,128]{3,2,1,0:T(8,128)(2,1)} collective-permute-done((bf16[2,32,128,128]{3,2,1,0:T(8,128)(2,1)}, bf16[2,32,128,128]{3,2,1,0:T(8,128)(2,1)}, u32[]{:S(2)}, u32[]{:S(2)}) %collective-permute-start) | collective-permute-done | bytes 2097184 | tf_op jit(solution)/shard_map/ppermute | solution.py:14
  61.2 45.1 %collective-permute-done.1 = bf16[2,32,128,128]{3,2,1,0:T(8,128)(2,1)} collective-permute-done((bf16[2,32,128,128]{3,2,1,0:T(8,128)(2,1)S(1)}, bf16[2,32,128,128]{3,2,1,0:T(8,128)(2,1)}, u32[]{:S(2)}, u32[]{:S(2)}) %collective-permute-start.1) | collective-permute-done | bytes 2097184 | tf_op jit(solution)/shard_map/ppermute | solution.py:14
  107.8 7.0 collective-permute-start.2
  117.8 40.5 %collective-permute-done.2 = bf16[2,32,128,128]{3,2,1,0:T(8,128)(2,1)S(1)} collective-permute-done((bf16[2,32,128,128]{3,2,1,0:T(8,128)(2,1)}, bf16[2,32,128,128]{3,2,1,0:T(8,128)(2,1)S(1)}, u32[]{:S(2)}, u32[]{:S(2)}) %collective-permute-start.2) | collective-permute-done | bytes 2097184 | tf_op jit(solution)/shard_map/ppermute | solution.py:14
  158.6 92.9 %while.42 = (s32[]{:T(128)}, f32[4096,64]{0,1:T(8,128)}, bf16[64,128,128]{2,1,0:T(8,128)(2,1)S(1)}, bf16[32,128,64]{2,1,0:T(8,128)(2,1)}, s32[]{:T(128)}, /*index=5*/s32[]{:T(128)}) while((s32[]{:T(128)}, f32[4096,64]{0,1:T(8,128)}, bf16[64,128,128]{2,1,0:T(8,128)(2,1)S(1)}, bf16[32,128,64]{2,1,0:T(8,128)(2,1)}, s32[]{:T(128)}, ...), condition=%wide.region_1.2_spmd.clone, body=%wide.region_0.1_spmd.clone.sunk | while | flops 67633152 | bytes 5276243 | solution.py:95
  251.6 81.7 %all-reduce.4.cloned.1.call-done = f32[4096,64]{0,1:T(8,128)} async-done(((f32[4096,64]{0,1:T(8,128)}), f32[4096,64]{0,1:T(8,128)}) %all-reduce.4.cloned.1.call-update) | async-done | bytes 1048592 | tf_op jit(solution)/shard_map/psum | solution.py:98
  335.9 11.3 %psum.29 = f32[64,64]{1,0:T(8,128)S(1)} all-reduce(f32[64,64]{1,0:T(8,128)S(1)} %fusion.39), channel_id=1, replica_groups=mesh['row'=4,'col'=8] {'row'}, use_global_device_ids=true, to_apply=%region_3.4 | all-reduce | flops 4096 | bytes 32768 | tf_op jit(solution)/shard_map/psum | solution.py:32
  359.6 39.2 %while.40 = (s32[]{:T(128)}, f32[64,4096]{1,0:T(8,128)}, bf16[64,128,128]{2,1,0:T(8,128)(2,1)S(1)}, bf16[4096,64]{1,0:T(8,128)(2,1)S(1)}, s32[]{:T(128)}, /*index=5*/s32[]{:T(128)}, s32[]{:T(128)}, s32[]{:T(128)}) while((s32[]{:T(128)}, f32[64,4096]{1,0:T(8,128)}, bf16[64,128,128]{2,1,0:T(8,128)(2,1)S(1)}, bf16[4096,64]{1,0:T(8,128)(2,1)S(1)}, ...), condition=%wide.region_6.7_spmd, body=%wide.region_5.6_spmd.sunk | while | flops 67108872 | bytes 3702923 | solution.py:107
  398.9 26.3 %all-reduce.7 = bf16[64,4096]{1,0:T(8,128)(2,1)S(1)} all-reduce(f32[64,4096]{1,0:T(8,128)} %get-tuple-element.243), channel_id=1, replica_groups=mesh['row'=4,'col'=8] {'row'}, use_global_device_ids=true, to_apply=%region_7.8 | all-reduce | flops 262144 | bytes 1572864 | tf_op jit(solution)/shard_map/psum | solution.py:110
  427.7 108.3 %while.41 = (s32[]{:T(128)}, f32[128,64,128]{2,0,1:T(8,128)}, bf16[32,128,64]{1,2,0:T(8,128)(2,1)}, bf16[64,4096]{1,0:T(8,128)(2,1)S(1)}, s32[]{:T(128)}) while((s32[]{:T(128)}, f32[128,64,128]{2,0,1:T(8,128)}, bf16[32,128,64]{1,2,0:T(8,128)(2,1)}, bf16[64,4096]{1,0:T(8,128)(2,1)S(1)}, s32[]{:T(128)}) %tuple.87), condition=%wide.region_9.10_spmd, body=%wide.region_8.9_spmd.sunk | while | flops 67633152 | bytes 4736061 | solution.py:63
  427.7 3.4 add_dynamic-update-slice_fusion.2
  431.1 3.4 add_dynamic-update-slice_fusion.2
  434.5 3.4 add_dynamic-update-slice_fusion.2
  437.9 3.4 add_dynamic-update-slice_fusion.2
  441.3 3.4 add_dynamic-update-slice_fusion.2
  444.7 3.4 add_dynamic-update-slice_fusion.2
  448.0 3.4 add_dynamic-update-slice_fusion.2
  451.4 3.4 add_dynamic-update-slice_fusion.2
  454.8 3.4 add_dynamic-update-slice_fusion.2
  458.2 3.4 add_dynamic-update-slice_fusion.2
  461.6 3.4 add_dynamic-update-slice_fusion.2
  465.0 3.4 add_dynamic-update-slice_fusion.2
  468.4 3.4 add_dynamic-update-slice_fusion.2
  471.7 3.4 add_dynamic-update-slice_fusion.2
  475.1 3.4 add_dynamic-update-slice_fusion.2
  478.5 3.4 add_dynamic-update-slice_fusion.2
  481.9 3.4 add_dynamic-update-slice_fusion.2
  485.3 3.4 add_dynamic-update-slice_fusion.2
  488.7 3.4 add_dynamic-update-slice_fusion.2
  492.1 3.4 add_dynamic-update-slice_fusion.2
  495.4 3.4 add_dynamic-update-slice_fusion.2
  498.8 3.4 add_dynamic-update-slice_fusion.2
  502.2 3.4 add_dynamic-update-slice_fusion.2
  505.6 3.4 add_dynamic-update-slice_fusion.2
  509.0 3.4 add_dynamic-update-slice_fusion.2
  512.4 3.4 add_dynamic-update-slice_fusion.2
  515.8 3.4 add_dynamic-update-slice_fusion.2
  519.1 3.4 add_dynamic-update-slice_fusion.2
  522.5 3.4 add_dynamic-update-slice_fusion.2
  525.9 3.4 add_dynamic-update-slice_fusion.2
  529.3 3.4 add_dynamic-update-slice_fusion.2
  532.7 3.4 add_dynamic-update-slice_fusion.2
  539.3 50.2 %collective-permute-done.3 = bf16[64,128,128]{2,1,0:T(8,128)(2,1)S(1)} collective-permute-done((bf16[64,128,128]{2,1,0:T(8,128)(2,1)S(1)}, bf16[64,128,128]{2,1,0:T(8,128)(2,1)S(1)}, u32[]{:S(2)}, u32[]{:S(2)}) %collective-permute-start.3) | collective-permute-done | bytes 2097184 | tf_op jit(solution)/shard_map/ppermute | solution.py:14
  590.2 48.9 %collective-permute-done.4 = bf16[64,128,128]{2,1,0:T(8,128)(2,1)S(1)} collective-permute-done((bf16[64,128,128]{2,1,0:T(8,128)(2,1)S(1)}, bf16[64,128,128]{2,1,0:T(8,128)(2,1)S(1)}, u32[]{:S(2)}, u32[]{:S(2)}) %collective-permute-start.4) | collective-permute-done | bytes 2097184 | tf_op jit(solution)/shard_map/ppermute | solution.py:14
  642.6 26.4 %collective-permute-done.5 = bf16[32,128,128]{2,1,0:T(8,128)(2,1)S(1)} collective-permute-done((bf16[32,128,128]{2,1,0:T(8,128)(2,1)S(1)}, bf16[32,128,128]{2,1,0:T(8,128)(2,1)S(1)}, u32[]{:S(2)}, u32[]{:S(2)}) %collective-permute-start.5) | collective-permute-done | bytes 1048608 | tf_op jit(solution)/shard_map/ppermute | solution.py:14
  673.6 81.6 %all-reduce.6.cloned.1.call-done = f32[2,32,128,128]{3,2,1,0:T(8,128)} async-done(((f32[2,32,128,128]{3,2,1,0:T(8,128)}), f32[2,32,128,128]{3,2,1,0:T(8,128)}) %all-reduce.6.cloned.1.call-update) | async-done | bytes 4194320 | tf_op jit(solution)/shard_map/psum | solution.py:129
  755.3 5.0 convert_select_fusion
  (193 shorter events, 168.3 us)
Async XLA Ops:
  6.5 326.8 %all-reduce.4.cloned.1.call-start = ((), (), s32[]{:S(2)}) async-start(), calls=%async_computation | async-start | bytes 2097152 | tf_op jit(solution)/shard_map/psum | solution.py:98
  6.5 51.2 %collective-permute-start = (bf16[2,32,128,128]{3,2,1,0:T(8,128)(2,1)}, bf16[2,32,128,128]{3,2,1,0:T(8,128)(2,1)}, u32[]{:S(2)}, u32[]{:S(2)}) collective-permute-start(bf16[2,32,128,128]{3,2,1,0:T(8,128)(2,1)} %param.8), channel_id=1, source_target_pairs={{1,0},{2,1},{3,2},{4,3},{5,4},{6,5},{7,6},{0,7},{9,8},{10,9},{11,1... | collective-permute-start | bytes 6291464 | tf_op jit(solution)/shard_map/ppermute | solution.py:14
  59.6 46.7 %collective-permute-start.1 = (bf16[2,32,128,128]{3,2,1,0:T(8,128)(2,1)S(1)}, bf16[2,32,128,128]{3,2,1,0:T(8,128)(2,1)}, u32[]{:S(2)}, u32[]{:S(2)}) collective-permute-start(bf16[2,32,128,128]{3,2,1,0:T(8,128)(2,1)S(1)} %broadcast_select_fusion), channel_id=1, source_target_pairs={{2,0},{3,1},{4,2},{5,3},{6,4},{7,5},{0,6},{1,7},{10,8},{11,9},{12,... | collective-permute-start | bytes 6291464 | tf_op jit(solution)/shard_map/ppermute | solution.py:14
  61.2 53.6 %copy-start.4 = (bf16[4096,64]{0,1:T(8,128)(2,1)S(1)}, bf16[4096,64]{0,1:T(8,128)(2,1)}, u32[]{:S(2)}) copy-start(bf16[4096,64]{0,1:T(8,128)(2,1)} %param.9) | copy-start | bytes 1572868
  107.8 50.5 %collective-permute-start.2 = (bf16[2,32,128,128]{3,2,1,0:T(8,128)(2,1)}, bf16[2,32,128,128]{3,2,1,0:T(8,128)(2,1)S(1)}, u32[]{:S(2)}, u32[]{:S(2)}) collective-permute-start(bf16[2,32,128,128]{3,2,1,0:T(8,128)(2,1)} %broadcast_select_fusion.1), channel_id=1, source_target_pairs={{1,0},{2,1},{3,2},{4,3},{5,4},{6,5},{7,6},{0,7},{9,8},{10,9},{11,1... | collective-permute-start | bytes 6291464 | tf_op jit(solution)/shard_map/ppermute | solution.py:14
  251.5 503.7 %all-reduce.6.cloned.1.call-start = ((), (), s32[]{:S(2)}) async-start(), calls=%async_computation.1 | async-start | bytes 8388608 | tf_op jit(solution)/shard_map/psum | solution.py:129
  333.3 19.9 %copy-start.2 = (f32[4096,64]{0,1:T(8,128)S(1)}, f32[4096,64]{0,1:T(8,128)}, u32[]{:S(2)}) copy-start(f32[4096,64]{0,1:T(8,128)} %all-reduce.4.cloned.1.call-done) | copy-start | bytes 3145732
  536.1 53.4 %copy-start = (f32[128,64,128]{2,0,1:T(8,128)S(1)}, f32[128,64,128]{2,0,1:T(8,128)}, u32[]{:S(2)}) copy-start(f32[128,64,128]{2,0,1:T(8,128)} %get-tuple-element.244) | copy-start | bytes 12582916
  538.8 50.7 %collective-permute-start.3 = (bf16[64,128,128]{2,1,0:T(8,128)(2,1)S(1)}, bf16[64,128,128]{2,1,0:T(8,128)(2,1)S(1)}, u32[]{:S(2)}, u32[]{:S(2)}) collective-permute-start(bf16[64,128,128]{2,1,0:T(8,128)(2,1)S(1)} %bitcast_convert_fusion), channel_id=1, source_target_pairs={{7,0},{0,1},{1,2},{2,3},{3,4},{4,5},{5,6},{6,7},{15,8},{8,9},{9,10... | collective-permute-start | bytes 6291464 | tf_op jit(solution)/shard_map/ppermute | solution.py:14
  590.1 48.9 %collective-permute-start.4 = (bf16[64,128,128]{2,1,0:T(8,128)(2,1)S(1)}, bf16[64,128,128]{2,1,0:T(8,128)(2,1)S(1)}, u32[]{:S(2)}, u32[]{:S(2)}) collective-permute-start(bf16[64,128,128]{2,1,0:T(8,128)(2,1)S(1)} %fusion.10), channel_id=1, source_target_pairs={{6,0},{7,1},{0,2},{1,3},{2,4},{3,5},{4,6},{5,7},{14,8},{15,9},{8,1... | collective-permute-start | bytes 6291464 | tf_op jit(solution)/shard_map/ppermute | solution.py:14
  640.3 2.0 copy-start.1
  642.4 26.5 %collective-permute-start.5 = (bf16[32,128,128]{2,1,0:T(8,128)(2,1)S(1)}, bf16[32,128,128]{2,1,0:T(8,128)(2,1)S(1)}, u32[]{:S(2)}, u32[]{:S(2)}) collective-permute-start(bf16[32,128,128]{2,1,0:T(8,128)(2,1)S(1)} %slice.43), channel_id=1, source_target_pairs={{7,0},{0,1},{1,2},{2,3},{3,4},{4,5},{5,6},{6,7},{15,8},{8,9},{9,10... | collective-permute-start | bytes 3145736 | tf_op jit(solution)/shard_map/ppermute | solution.py:14
  673.5 81.8 %copy-start.3 = (bf16[2,32,128,128]{3,2,1,0:T(8,128)(2,1)S(1)}, bf16[2,32,128,128]{3,2,1,0:T(8,128)(2,1)}, u32[]{:S(2)}) copy-start(bf16[2,32,128,128]{3,2,1,0:T(8,128)(2,1)} %param.8) | copy-start | bytes 6291460
Sparse Core Ops, SparseCore 0:
  251.7 81.5 all-reduce.3
  673.6 81.6 all-reduce.5
where the time goes:
time: 770 us; the launch traced here: 767 us
  waiting for transfers between devices  420 us (55%)
  matrix products  242 us (31%)
  blocking collectives  37.7 us (5%)
  other arithmetic  20.1 us (3%)
  local copies, waits for them, and re-layouts  17 us (2%)
  starting transfers between devices  15.3 us (2%)
  between operations  14.5 us (2%)
    ppermute x6, waiting for transfers between devices, shifted(): return lax.ppermute(block, axis, route)  256 us
    dot_general x32, matrix products, add_row(): jnp.dot(orthonormal_row_vector, column_rows, preferred_element_type=jnp.f...  108 us
    dot_general x32, matrix products, range_step(): jnp.dot(slab_at(column_id), weights, preferred_element_type=jnp.float32)  89.3 us
    psum x1, waiting for transfers between devices, local(): sketch = lax.psum(partial_value, 'col')  81.7 us
    psum x1, waiting for transfers between devices, local(): totals = lax.psum(owned, 'row')  81.6 us
    dot_general x32, matrix products, projection_update(): lax.dot_general(basis, slab_at(column_id), (((0,), (0,)), ((), ())), pref...  35.7 us
    psum x1, blocking collectives, local(): projected_matrix = lax.psum(projected_matrix, 'row').astype(jnp.bfloat16)  26.3 us
  transfers between devices with their start and end apart: 8, of which 8 were waited for; matrix products, arithmetic and copies ran while one was open for 0% of the time, Pallas kernels for 0%

commit v1 on v0

--- a/solution.py
+++ b/solution.py
@@ -95,7 +95,7 @@
     partial_value = lax.fori_loop(
         0, blocks, range_step, jnp.zeros((blocks * out_rows, rank_extent), jnp.float32)
     )
-    sketch = lax.psum(partial_value, "col")
+    sketch = jnp.sum(lax.all_gather(partial_value, "col"), axis=0)
     basis = orthonormal(sketch).astype(jnp.bfloat16)
 
     def projection_update(column_id, running):

time: 770 us -> 825 us (1.071)
  waiting for transfers between devices: 420 us -> 467 us
    all_gather x0 -> x1, waiting for transfers between devices: none -> 128 us  [local(): sketch = jnp.sum(lax.all_gather(partial_value, 'col'), axis=0)]
    psum x1 -> x0, waiting for transfers between devices: 81.7 us -> none  [local(): sketch = lax.psum(partial_value, 'col')]
where the time goes in v1:
time: 825 us; the launch traced here: 822 us
  waiting for transfers between devices  467 us (57%)
  matrix products  241 us (29%)
  blocking collectives  36.9 us (4%)
  local copies, waits for them, and re-layouts  25.1 us (3%)
  other arithmetic  22.2 us (3%)
  starting transfers between devices  15.4 us (2%)
  between operations  14.5 us (2%)
    ppermute x6, waiting for transfers between devices, shifted(): return lax.ppermute(block, axis, route)  256 us
    all_gather x1, waiting for transfers between devices, local(): sketch = jnp.sum(lax.all_gather(partial_value, 'col'), axis=0)  128 us
    dot_general x32, matrix products, add_row(): jnp.dot(orthonormal_row_vector, column_rows, preferred_element_type=jnp.f...  108 us
    dot_general x32, matrix products, range_step(): jnp.dot(slab_at(column_id), weights, preferred_element_type=jnp.float32)  89.2 us
    psum x1, waiting for transfers between devices, local(): totals = lax.psum(owned, 'row')  82.6 us
    dot_general x32, matrix products, projection_update(): lax.dot_general(basis, slab_at(column_id), (((0,), (0,)), ((), ())), pref...  35.7 us
    psum x1, blocking collectives, local(): projected_matrix = lax.psum(projected_matrix, 'row').astype(jnp.bfloat16)  26.4 us
  transfers between devices with their start and end apart: 8, of which 8 were waited for; matrix products, arithmetic and copies ran while one was open for 0% of the time, Pallas kernels for 0%

profile of v1, /device:TPU:0, one launch (start us, length us, event | category | flops | bytes accessed | tf_op | source)
XLA Modules:
  0.0 822.0 jit_solution(9660652616724607382)
XLA Ops:
  6.5 6.0 collective-permute-start
  12.6 45.2 %collective-permute-done = bf16[2,32,128,128]{3,2,1,0:T(8,128)(2,1)} collective-permute-done((bf16[2,32,128,128]{3,2,1,0:T(8,128)(2,1)}, bf16[2,32,128,128]{3,2,1,0:T(8,128)(2,1)}, u32[]{:S(2)}, u32[]{:S(2)}) %collective-permute-start) | collective-permute-done | bytes 2097184 | tf_op jit(solution)/shard_map/ppermute | solution.py:14
  61.2 45.1 %collective-permute-done.1 = bf16[2,32,128,128]{3,2,1,0:T(8,128)(2,1)} collective-permute-done((bf16[2,32,128,128]{3,2,1,0:T(8,128)(2,1)S(1)}, bf16[2,32,128,128]{3,2,1,0:T(8,128)(2,1)}, u32[]{:S(2)}, u32[]{:S(2)}) %collective-permute-start.1) | collective-permute-done | bytes 2097184 | tf_op jit(solution)/shard_map/ppermute | solution.py:14
  107.8 7.0 collective-permute-start.2
  117.8 40.5 %collective-permute-done.2 = bf16[2,32,128,128]{3,2,1,0:T(8,128)(2,1)S(1)} collective-permute-done((bf16[2,32,128,128]{3,2,1,0:T(8,128)(2,1)}, bf16[2,32,128,128]{3,2,1,0:T(8,128)(2,1)S(1)}, u32[]{:S(2)}, u32[]{:S(2)}) %collective-permute-start.2) | collective-permute-done | bytes 2097184 | tf_op jit(solution)/shard_map/ppermute | solution.py:14
  158.6 92.9 %while.42 = (s32[]{:T(128)}, f32[4096,64]{0,1:T(8,128)}, bf16[64,128,128]{2,1,0:T(8,128)(2,1)S(1)}, bf16[32,128,64]{2,1,0:T(8,128)(2,1)}, s32[]{:T(128)}, /*index=5*/s32[]{:T(128)}) while((s32[]{:T(128)}, f32[4096,64]{0,1:T(8,128)}, bf16[64,128,128]{2,1,0:T(8,128)(2,1)S(1)}, bf16[32,128,64]{2,1,0:T(8,128)(2,1)}, s32[]{:T(128)}, ...), condition=%wide.region_1.2_spmd.clone, body=%wide.region_0.1_spmd.clone.sunk | while | flops 67633152 | bytes 5276243 | solution.py:95
  251.5 127.9 %all-gather.3.cloned.1.call-done = f32[32768,64]{0,1:T(8,128)} async-done(((f32[4096,64]{0,1:T(8,128)}), f32[32768,64]{0,1:T(8,128)}) %all-gather.3.cloned.1.call-update) | async-done | bytes 8388624 | tf_op jit(solution)/shard_map/all_gather | solution.py:98
  379.4 8.1 copy.13
  390.6 10.4 %psum.21 = f32[64,64]{1,0:T(8,128)S(1)} all-reduce(f32[64,64]{1,0:T(8,128)S(1)} %fusion.39), channel_id=1, replica_groups=mesh['row'=4,'col'=8] {'row'}, use_global_device_ids=true, to_apply=%region_3.4 | all-reduce | flops 4096 | bytes 32768 | tf_op jit(solution)/shard_map/psum | solution.py:32
  413.5 39.2 %while.40 = (s32[]{:T(128)}, f32[64,4096]{1,0:T(8,128)}, bf16[64,128,128]{2,1,0:T(8,128)(2,1)S(1)}, bf16[4096,64]{1,0:T(8,128)(2,1)S(1)}, s32[]{:T(128)}, /*index=5*/s32[]{:T(128)}, s32[]{:T(128)}, s32[]{:T(128)}) while((s32[]{:T(128)}, f32[64,4096]{1,0:T(8,128)}, bf16[64,128,128]{2,1,0:T(8,128)(2,1)S(1)}, bf16[4096,64]{1,0:T(8,128)(2,1)S(1)}, ...), condition=%wide.region_6.7_spmd, body=%wide.region_5.6_spmd.sunk | while | flops 67108872 | bytes 3702923 | solution.py:107
  452.7 26.4 %all-reduce.4 = bf16[64,4096]{1,0:T(8,128)(2,1)S(1)} all-reduce(f32[64,4096]{1,0:T(8,128)} %get-tuple-element.243), channel_id=1, replica_groups=mesh['row'=4,'col'=8] {'row'}, use_global_device_ids=true, to_apply=%region_7.8 | all-reduce | flops 262144 | bytes 1572864 | tf_op jit(solution)/shard_map/psum | solution.py:110
  481.6 108.3 %while.41 = (s32[]{:T(128)}, f32[128,64,128]{2,0,1:T(8,128)}, bf16[32,128,64]{1,2,0:T(8,128)(2,1)}, bf16[64,4096]{1,0:T(8,128)(2,1)S(1)}, s32[]{:T(128)}) while((s32[]{:T(128)}, f32[128,64,128]{2,0,1:T(8,128)}, bf16[32,128,64]{1,2,0:T(8,128)(2,1)}, bf16[64,4096]{1,0:T(8,128)(2,1)S(1)}, s32[]{:T(128)}) %tuple.89), condition=%wide.region_9.10_spmd, body=%wide.region_8.9_spmd.sunk | while | flops 67633152 | bytes 4736061 | solution.py:63
  485.0 3.4 add_dynamic-update-slice_fusion.2
  488.4 3.4 add_dynamic-update-slice_fusion.2
  491.8 3.4 add_dynamic-update-slice_fusion.2
  495.2 3.4 add_dynamic-update-slice_fusion.2
  498.6 3.4 add_dynamic-update-slice_fusion.2
  502.0 3.4 add_dynamic-update-slice_fusion.2
  505.3 3.4 add_dynamic-update-slice_fusion.2
  508.7 3.4 add_dynamic-update-slice_fusion.2
  512.1 3.4 add_dynamic-update-slice_fusion.2
  515.5 3.4 add_dynamic-update-slice_fusion.2
  518.9 3.4 add_dynamic-update-slice_fusion.2
  522.3 3.4 add_dynamic-update-slice_fusion.2
  525.7 3.4 add_dynamic-update-slice_fusion.2
  529.0 3.4 add_dynamic-update-slice_fusion.2
  532.4 3.4 add_dynamic-update-slice_fusion.2
  535.8 3.4 add_dynamic-update-slice_fusion.2
  539.2 3.4 add_dynamic-update-slice_fusion.2
  542.6 3.4 add_dynamic-update-slice_fusion.2
  546.0 3.4 add_dynamic-update-slice_fusion.2
  549.3 3.4 add_dynamic-update-slice_fusion.2
  552.7 3.4 add_dynamic-update-slice_fusion.2
  556.1 3.4 add_dynamic-update-slice_fusion.2
  559.5 3.4 add_dynamic-update-slice_fusion.2
  562.9 3.4 add_dynamic-update-slice_fusion.2
  566.3 3.4 add_dynamic-update-slice_fusion.2
  569.7 3.4 add_dynamic-update-slice_fusion.2
  573.0 3.4 add_dynamic-update-slice_fusion.2
  576.4 3.4 add_dynamic-update-slice_fusion.2
  579.8 3.4 add_dynamic-update-slice_fusion.2
  583.2 3.4 add_dynamic-update-slice_fusion.2
  586.6 3.4 add_dynamic-update-slice_fusion.2
  593.3 50.1 %collective-permute-done.3 = bf16[64,128,128]{2,1,0:T(8,128)(2,1)S(1)} collective-permute-done((bf16[64,128,128]{2,1,0:T(8,128)(2,1)S(1)}, bf16[64,128,128]{2,1,0:T(8,128)(2,1)S(1)}, u32[]{:S(2)}, u32[]{:S(2)}) %collective-permute-start.3) | collective-permute-done | bytes 2097184 | tf_op jit(solution)/shard_map/ppermute | solution.py:14
  644.1 48.9 %collective-permute-done.4 = bf16[64,128,128]{2,1,0:T(8,128)(2,1)S(1)} collective-permute-done((bf16[64,128,128]{2,1,0:T(8,128)(2,1)S(1)}, bf16[64,128,128]{2,1,0:T(8,128)(2,1)S(1)}, u32[]{:S(2)}, u32[]{:S(2)}) %collective-permute-start.4) | collective-permute-done | bytes 2097184 | tf_op jit(solution)/shard_map/ppermute | solution.py:14
  696.5 26.4 %collective-permute-done.5 = bf16[32,128,128]{2,1,0:T(8,128)(2,1)S(1)} collective-permute-done((bf16[32,128,128]{2,1,0:T(8,128)(2,1)S(1)}, bf16[32,128,128]{2,1,0:T(8,128)(2,1)S(1)}, u32[]{:S(2)}, u32[]{:S(2)}) %collective-permute-start.5) | collective-permute-done | bytes 1048608 | tf_op jit(solution)/shard_map/ppermute | solution.py:14
  727.6 82.6 %all-reduce.3.cloned.1.call-done = f32[2,32,128,128]{3,2,1,0:T(8,128)} async-done(((f32[2,32,128,128]{3,2,1,0:T(8,128)}), f32[2,32,128,128]{3,2,1,0:T(8,128)}) %all-reduce.3.cloned.1.call-update) | async-done | bytes 4194320 | tf_op jit(solution)/shard_map/psum | solution.py:129
  810.1 5.0 convert_select_fusion
  (193 shorter events, 172.2 us)
Async XLA Ops:
  6.5 372.9 %all-gather.3.cloned.1.call-start = ((), (), s32[]{:S(2)}) async-start(), calls=%async_computation.1 | async-start | bytes 9437184 | tf_op jit(solution)/shard_map/all_gather | solution.py:98
  6.5 51.2 %collective-permute-start = (bf16[2,32,128,128]{3,2,1,0:T(8,128)(2,1)}, bf16[2,32,128,128]{3,2,1,0:T(8,128)(2,1)}, u32[]{:S(2)}, u32[]{:S(2)}) collective-permute-start(bf16[2,32,128,128]{3,2,1,0:T(8,128)(2,1)} %param.8), channel_id=1, source_target_pairs={{1,0},{2,1},{3,2},{4,3},{5,4},{6,5},{7,6},{0,7},{9,8},{10,9},{11,1... | collective-permute-start | bytes 6291464 | tf_op jit(solution)/shard_map/ppermute | solution.py:14
  59.6 46.7 %collective-permute-start.1 = (bf16[2,32,128,128]{3,2,1,0:T(8,128)(2,1)S(1)}, bf16[2,32,128,128]{3,2,1,0:T(8,128)(2,1)}, u32[]{:S(2)}, u32[]{:S(2)}) collective-permute-start(bf16[2,32,128,128]{3,2,1,0:T(8,128)(2,1)S(1)} %broadcast_select_fusion), channel_id=1, source_target_pairs={{2,0},{3,1},{4,2},{5,3},{6,4},{7,5},{0,6},{1,7},{10,8},{11,9},{12,... | collective-permute-start | bytes 6291464 | tf_op jit(solution)/shard_map/ppermute | solution.py:14
  61.2 53.6 %copy-start.3 = (bf16[4096,64]{0,1:T(8,128)(2,1)S(1)}, bf16[4096,64]{0,1:T(8,128)(2,1)}, u32[]{:S(2)}) copy-start(bf16[4096,64]{0,1:T(8,128)(2,1)} %param.9) | copy-start | bytes 1572868
  107.8 50.5 %collective-permute-start.2 = (bf16[2,32,128,128]{3,2,1,0:T(8,128)(2,1)}, bf16[2,32,128,128]{3,2,1,0:T(8,128)(2,1)S(1)}, u32[]{:S(2)}, u32[]{:S(2)}) collective-permute-start(bf16[2,32,128,128]{3,2,1,0:T(8,128)(2,1)} %broadcast_select_fusion.1), channel_id=1, source_target_pairs={{1,0},{2,1},{3,2},{4,3},{5,4},{6,5},{7,6},{0,7},{9,8},{10,9},{11,1... | collective-permute-start | bytes 6291464 | tf_op jit(solution)/shard_map/ppermute | solution.py:14
  251.5 558.7 %all-reduce.3.cloned.1.call-start = ((), (), s32[]{:S(2)}) async-start(), calls=%async_computation | async-start | bytes 8388608 | tf_op jit(solution)/shard_map/psum | solution.py:129
  590.0 53.4 %copy-start = (f32[128,64,128]{2,0,1:T(8,128)S(1)}, f32[128,64,128]{2,0,1:T(8,128)}, u32[]{:S(2)}) copy-start(f32[128,64,128]{2,0,1:T(8,128)} %get-tuple-element.244) | copy-start | bytes 12582916
  592.7 50.7 %collective-permute-start.3 = (bf16[64,128,128]{2,1,0:T(8,128)(2,1)S(1)}, bf16[64,128,128]{2,1,0:T(8,128)(2,1)S(1)}, u32[]{:S(2)}, u32[]{:S(2)}) collective-permute-start(bf16[64,128,128]{2,1,0:T(8,128)(2,1)S(1)} %bitcast_convert_fusion), channel_id=1, source_target_pairs={{7,0},{0,1},{1,2},{2,3},{3,4},{4,5},{5,6},{6,7},{15,8},{8,9},{9,10... | collective-permute-start | bytes 6291464 | tf_op jit(solution)/shard_map/ppermute | solution.py:14
  644.0 48.9 %collective-permute-start.4 = (bf16[64,128,128]{2,1,0:T(8,128)(2,1)S(1)}, bf16[64,128,128]{2,1,0:T(8,128)(2,1)S(1)}, u32[]{:S(2)}, u32[]{:S(2)}) collective-permute-start(bf16[64,128,128]{2,1,0:T(8,128)(2,1)S(1)} %fusion.10), channel_id=1, source_target_pairs={{6,0},{7,1},{0,2},{1,3},{2,4},{3,5},{4,6},{5,7},{14,8},{15,9},{8,1... | collective-permute-start | bytes 6291464 | tf_op jit(solution)/shard_map/ppermute | solution.py:14
  694.2 2.0 copy-start.1
  696.4 26.5 %collective-permute-start.5 = (bf16[32,128,128]{2,1,0:T(8,128)(2,1)S(1)}, bf16[32,128,128]{2,1,0:T(8,128)(2,1)S(1)}, u32[]{:S(2)}, u32[]{:S(2)}) collective-permute-start(bf16[32,128,128]{2,1,0:T(8,128)(2,1)S(1)} %slice.43), channel_id=1, source_target_pairs={{7,0},{0,1},{1,2},{2,3},{3,4},{4,5},{5,6},{6,7},{15,8},{8,9},{9,10... | collective-permute-start | bytes 3145736 | tf_op jit(solution)/shard_map/ppermute | solution.py:14
  727.4 82.8 %copy-start.2 = (bf16[2,32,128,128]{3,2,1,0:T(8,128)(2,1)S(1)}, bf16[2,32,128,128]{3,2,1,0:T(8,128)(2,1)}, u32[]{:S(2)}) copy-start(bf16[2,32,128,128]{3,2,1,0:T(8,128)(2,1)} %param.8) | copy-start | bytes 6291460
Sparse Core Ops, SparseCore 0:
  251.6 127.8 all-gather.2
  727.5 82.5 all-reduce.2
